TPU v7x, 256 devices: a whole 4x4x8 slice. The times are simulated.
256 devices in a mesh: occ: 8 (over y_lo, x), vir: 32 (over y_hi, z, core).
Axes of the slice: x: 4, y: 4 (y_hi: 2, y_lo: 2; y = y_hi * 2 + y_lo), z: 8, core: 2. Of those that a mesh axis runs over, the one named last changes fastest.
Arguments:
- factors: bfloat16 [256, 1024, 2048], P(None, 'vir', 'occ'), may hold values from -0.125 to 0.125
- e_occ: float32 [256], replicated, may hold values from -2 to -0.3
- e_vir: float32 [1024], replicated, may hold values from 0.1 to 3
- i_sub: int32 [3], replicated, may hold values from 0 to 1
- j_row: int32 [3], replicated, may hold values from 0 to 255
Outputs:
- density: float32 [256, 1024, 2048], P(None, 'vir', 'occ')
All inputs are finite; a program needn't handle non-finite values.
Results may differ from a plain program's by a relative error of at most 0.0022.
Values may be sent and summed in bfloat16 or wider, within the bound.
A program may use at most 128 MiB of HBM per device.

v0:
```python
import jax
import jax.numpy as jnp
from jax import lax
from jax.sharding import PartitionSpec as P

IBK = 16
STEPS = 3


def from_root(shard, axis, root):
    mine = lax.axis_index(axis) == root
    return lax.psum(jnp.where(mine, shard, jnp.zeros_like(shard)), axis)


def pair_terms(accumulator, row_block, energy_rows, energy_own, energy_pair, column_piece, e_vir):
    integrals = jnp.einsum(
        "iap,bp->iab", row_block, column_piece, preferred_element_type=jnp.float32
    )
    denominator = (
        energy_own[None, :, None] + e_vir[None, None, :] - energy_rows[:, None, None] - energy_pair
    )
    amplitude = (-integrals / denominator).astype(jnp.bfloat16)
    return accumulator + jnp.einsum(
        "iab,bp->iap", amplitude, column_piece, preferred_element_type=jnp.float32
    )


def shards(factors, e_occ, e_vir, i_sub, j_row):
    regrouped = lax.all_to_all(factors, "occ", split_axis=0, concat_axis=2, tiled=True)
    owned, vir_own, aux_total = regrouped.shape
    occ_rank = lax.axis_index("occ")
    vir_rank = lax.axis_index("vir")
    energy_own = lax.dynamic_slice_in_dim(e_vir, vir_rank * vir_own, vir_own, 0)
    density = jnp.zeros((owned, vir_own, aux_total), jnp.float32)
    offsets = []
    row_blocks = []
    energy_list = []
    pair_slabs = []
    pair_energies = []
    for step_index in range(STEPS):
        offset = i_sub[step_index] * IBK
        j_index = j_row[step_index]
        owner = j_index // owned
        own_slab = lax.dynamic_index_in_dim(regrouped, j_index % owned, 0, keepdims=False)
        pair_slab = from_root(own_slab, "occ", owner)
        offsets.append(offset)
        row_blocks.append(lax.dynamic_slice_in_dim(regrouped, offset, IBK, 0))
        energy_list.append(lax.dynamic_slice_in_dim(e_occ, occ_rank * owned + offset, IBK, 0))
        pair_slabs.append(pair_slab)
        pair_energies.append(e_occ[j_index])
    for step_index in range(STEPS):
        previous = lax.dynamic_slice_in_dim(density, offsets[step_index], IBK, 0)
        updated = pair_terms(
            previous,
            row_blocks[step_index],
            energy_list[step_index],
            energy_own,
            pair_energies[step_index],
            lax.all_gather(pair_slabs[step_index], "vir", axis=0, tiled=True),
            e_vir,
        )
        density = lax.dynamic_update_slice_in_dim(density, updated, offsets[step_index], 0)
    return lax.all_to_all(density, "occ", split_axis=2, concat_axis=0, tiled=True)


def solution(mesh):
    placed = (P(None, "vir", "occ"), P(), P(), P(), P())
    return jax.shard_map(
        shards, mesh=mesh, in_specs=placed, out_specs=P(None, "vir", "occ"), check_vma=False
    )
```

profile of v0, /device:TPU:1, one launch (start us, length us, event | category | flops | bytes accessed | tf_op | source)
XLA Modules:
  0.0 679.4 jit_solution(2114121080004834413)
XLA Ops:
  6.5 6.0 all-to-all-start
  12.6 0.6 fusion.64
  20.4 41.8 %all-to-all-done = bf16[256,32,256]{2,1,0:T(8,128)(2,1)} async-done(((bf16[256,32,256]{2,1,0:T(8,128)(2,1)}), bf16[256,32,256]{2,1,0:T(8,128)(2,1)}, u32[]{:S(2)}, u32[]{:S(2)}) %all-to-all-start) | async-done | bytes 4194336 | tf_op jit(solution)/shard_map/all_to_all | solution.py:29
  62.2 8.5 %copy.12 = bf16[8,32,32,256]{3,0,2,1:T(8,128)(2,1)} copy(bf16[8,32,32,256]{3,2,1,0:T(8,128)(2,1)} %bitcast) | data formatting | bytes 8388608 | tf_op jit(solution)/shard_map/all_to_all | solution.py:29
  70.7 7.4 %all_to_all.29 = bf16[32,32,2048]{2,1,0:T(8,128)(2,1)} reshape(bf16[32,32,8,256]{3,2,1,0:T(8,128)(2,1)} %bitcast.62) | data formatting | bytes 8388608 | tf_op jit(solution)/shard_map/all_to_all | solution.py:29
  78.1 1.8 select_bitcast_fusion
  80.0 89.0 %all-reduce.3.cloned.1.call-done = (bf16[32,2048]{1,0:T(8,128)(2,1)}, bf16[32,2048]{1,0:T(8,128)(2,1)}, bf16[32,2048]{1,0:T(8,128)(2,1)}) async-done(((bf16[32,2048]{1,0:T(8,128)(2,1)}, bf16[32,2048]{1,0:T(8,128)(2,1)}, bf16[32,2048]{1,0:T(8,128)(2,1)}), (bf16[32,2048]{1,0:T(8,128)(2,1)}, bf16[32,2048]{1,0:T(8,128)(2,1)}, bf16[32,2048]{1,0:T(8,128)(2,1)})) %all-reduce.3.cloned.1.call-update) | async-done | bytes 393232 | tf_op jit(solution)/shard_map/psum | solution.py:12
  169.1 0.7 all-gather.6.cloned.1.call-update
  170.3 0.7 fusion.63
  176.5 0.6 fusion.62
  177.3 86.9 %all-gather.4.cloned.1.call-done = bf16[1024,2048]{1,0:T(8,128)(2,1)} async-done(((bf16[32,2048]{1,0:T(8,128)(2,1)}), bf16[1024,2048]{1,0:T(8,128)(2,1)}) %all-gather.4.cloned.1.call-update) | async-done | bytes 4194320 | tf_op jit(solution)/shard_map/all_gather | solution.py:59
  264.1 4.5 broadcast_in_dim.2
  268.6 11.2 %fusion.12 = f32[32,32,2048]{2,1,0:T(8,128)} fusion(f32[32,32,2048]{2,1,0:T(8,128)} %broadcast_in_dim.2, s32[]{:T(128)S(6)} %select_n.99, bf16[1024,2048]{1,0:T(8,128)(2,1)} %all-gather.4.cloned.1.call-done, bf16[32,32,2048]{2,1,0:T(8,128)(2,1)} %all_to_all.29, f32[]{:T(128)} %bitcast.6, f32[16]{0:T(128)S(1)} %get-tuple-element.13, ...), kind=kOutput, calls=%fused_computation.15 | convolution fusion | flops 4297588736 | bytes 14812736 | tf_op jit(solution)/shard_map/iab,bp->iap/dot_general | solution.py:23
  279.8 70.5 %all-gather.6.cloned.1.call-done = bf16[1024,2048]{1,0:T(8,128)(2,1)} async-done(((bf16[32,2048]{1,0:T(8,128)(2,1)}), bf16[1024,2048]{1,0:T(8,128)(2,1)}) %all-gather.6.cloned.1.call-update) | async-done | bytes 4194320 | tf_op jit(solution)/shard_map/all_gather | solution.py:59
  350.2 12.4 %add_dynamic-update-slice_fusion.1 = f32[32,32,2048]{2,1,0:T(8,128)} fusion(f32[32,32,2048]{2,1,0:T(8,128)} %fusion.12, s32[]{:T(128)S(6)} %select_n.109, bf16[1024,2048]{1,0:T(8,128)(2,1)} %all-gather.6.cloned.1.call-done, bf16[32,32,2048]{2,1,0:T(8,128)(2,1)} %all_to_all.29, f32[]{:T(128)} %bitcast.11, f32[16]{0:T(128)S(1)} %get-tuple-element.12, ...), kind=kOutput, calls=%fused_computation.14 | convolution fusion | flops 4298637312 | bytes 19007040 | tf_op jit(solution)/shard_map/iab,bp->iap/dot_general | solution.py:23
  362.7 73.5 %all-gather.8.cloned.1.call-done = bf16[1024,2048]{1,0:T(8,128)(2,1)} async-done(((bf16[32,2048]{1,0:T(8,128)(2,1)}), bf16[1024,2048]{1,0:T(8,128)(2,1)}) %all-gather.8.cloned.1.call-update) | async-done | bytes 4194320 | tf_op jit(solution)/shard_map/all_gather | solution.py:59
  436.2 12.5 %add_dynamic-update-slice_fusion = f32[32,32,2048]{2,1,0:T(8,128)} fusion(f32[32,32,2048]{2,1,0:T(8,128)} %add_dynamic-update-slice_fusion.1, s32[]{:T(128)S(6)} %select_n.118, bf16[1024,2048]{1,0:T(8,128)(2,1)} %all-gather.8.cloned.1.call-done, bf16[32,32,2048]{2,1,0:T(8,128)(2,1)} %all_to_all.29, f32[]{:T(128)} %bitcast.16, f32[16]{0:T(128)S(1)} %get-tuple-element.11, ...), kind=kOutput, calls=%fused_computation.13 | convolution fusion | flops 4298637312 | bytes 19007040 | tf_op jit(solution)/shard_map/iab,bp->iap/dot_general | solution.py:23
  448.6 26.3 %copy.9 = f32[32,32,2048]{1,0,2:T(8,128)} copy(f32[32,32,2048]{2,1,0:T(8,128)} %add_dynamic-update-slice_fusion) | data formatting | bytes 16777216 | tf_op jit(solution)/shard_map/dynamic_update_slice | solution.py:62
  474.9 20.5 %reshape.53 = f32[8,1,262144]{2,1,0:T(1,128)} reshape(f32[2048,32,32]{2,1,0:T(8,128)} %bitcast.60) | data formatting | bytes 16777216
  495.4 100.2 %all_to_all.36 = f32[8,1,262144]{2,1,0:T(1,128)} all-to-all(f32[8,1,262144]{2,1,0:T(1,128)} %reshape.53), channel_id=1, replica_groups=mesh['occ'=8,'vir'=32] {'occ'}, dimensions={0} | all-to-all | bytes 16777216 | tf_op jit(solution)/shard_map/all_to_all | solution.py:63
  595.7 0.5 broadcast.49
  596.2 26.4 %reduce = f32[8,262144]{1,0:T(8,128)} reduce(f32[8,1,262144]{2,1,0:T(1,128)} %all_to_all.36, f32[]{:T(128)} %broadcast.49), dimensions={1}, to_apply=%all_to_all.30.reduce_sub_computation | reduce | bytes 16777220 | tf_op jit(solution)/shard_map/all_to_all | solution.py:63
  622.6 25.3 %reshape.54 = f32[2048,32,32]{2,1,0:T(8,128)} reshape(f32[8,262144]{1,0:T(8,128)} %reduce) | data formatting | bytes 16777216
  647.9 25.1 %copy.10 = f32[8,32,32,256]{3,2,1,0:T(8,128)} copy(f32[8,32,32,256]{2,1,3,0:T(8,128)} %bitcast.61) | data formatting | bytes 16777216 | tf_op jit(solution)/shard_map/all_to_all | solution.py:63
  (18 shorter events, 1.0 us)
Async XLA Ops:
  6.5 6.0 copy-start.1
  6.5 55.7 %all-to-all-start = ((bf16[256,32,256]{2,1,0:T(8,128)(2,1)}), bf16[256,32,256]{2,1,0:T(8,128)(2,1)}, u32[]{:S(2)}, u32[]{:S(2)}) async-start(bf16[256,32,256]{2,1,0:T(8,128)(2,1)} %param.5), calls=%async_computation | async-start | bytes 8388608 | tf_op jit(solution)/shard_map/all_to_all | solution.py:29
  12.5 156.5 %all-reduce.3.cloned.1.call-start = ((), (), s32[]{:S(2)}) async-start(), calls=%async_computation.5 | async-start | bytes 786432 | tf_op jit(solution)/shard_map/psum | solution.py:12
  70.7 99.7 %copy-start.2 = (s32[3]{0:T(128)S(1)}, s32[3]{0:T(128)}, u32[]{:S(2)}) copy-start(s32[3]{0:T(128)} %param.8) | copy-start | bytes 40
  70.7 105.7 %copy-start.3 = (f32[1024]{0:T(1024)S(1)}, f32[1024]{0:T(1024)}, u32[]{:S(2)}) copy-start(f32[1024]{0:T(1024)} %param.7) | copy-start | bytes 12292
  70.7 105.8 %copy-start = (f32[256]{0:T(256)S(1)}, f32[256]{0:T(256)}, u32[]{:S(2)}) copy-start(f32[256]{0:T(256)} %param.6) | copy-start | bytes 3076
  79.9 184.2 %all-gather.4.cloned.1.call-start = ((), (), s32[]{:S(2)}) async-start(), calls=%async_computation.2 | async-start | bytes 4325376 | tf_op jit(solution)/shard_map/all_gather | solution.py:59
  169.0 181.2 %all-gather.6.cloned.1.call-start = ((), (), s32[]{:S(2)}) async-start(), calls=%async_computation.3 | async-start | bytes 4325376 | tf_op jit(solution)/shard_map/all_gather | solution.py:59
  169.8 266.4 %all-gather.8.cloned.1.call-start = ((), (), s32[]{:S(2)}) async-start(), calls=%async_computation.4 | async-start | bytes 4325376 | tf_op jit(solution)/shard_map/all_gather | solution.py:59
Sparse Core Ops, SparseCore 0:
  80.0 88.8 all-reduce.2
  171.8 92.3 all-gather.3
  266.9 83.2 all-gather.5
  352.9 83.2 all-gather.7
where the time goes:
time: 681 us; the launch traced here: 679 us
  waiting for transfers between devices  363 us (53%)
  local copies, waits for them, and re-layouts  120 us (18%)
  blocking collectives  100 us (15%)
  matrix products  36.1 us (5%)
  other arithmetic  28.3 us (4%)
  between operations  25.8 us (4%)
    all_gather x3, waiting for transfers between devices, shards(): lax.all_gather(pair_slabs[step_index], 'vir', axis=0, tiled=True)  231 us
    all_to_all x1, blocking collectives, shards(): lax.all_to_all(density, 'occ', split_axis=2, concat_axis=0, tiled=True)  100 us
    psum x1, waiting for transfers between devices, from_root(): return lax.psum(jnp.where(mine, shard, jnp.zeros_like(shard)), axis)  89 us
    unnamed x10, local copies, waits for them, and re-layouts  45.8 us
    all_to_all x1, waiting for transfers between devices, shards(): lax.all_to_all(factors, 'occ', split_axis=0, concat_axis=2, tiled=True)  41.8 us
    dot_general x3, matrix products, pair_terms(): jnp.einsum('iab,bp->iap', amplitude, column_piece, preferred_element_type...  36.1 us
    all_to_all x1, other arithmetic, shards(): lax.all_to_all(density, 'occ', split_axis=2, concat_axis=0, tiled=True)  26.4 us
    dynamic_update_slice x1, local copies, waits for them, and re-layouts, shards(): lax.dynamic_update_slice_in_dim(density, updated, offsets[step_index], 0)  26.3 us
  transfers between devices with their start and end apart: 5, of which 5 were waited for; matrix products, arithmetic and copies ran while one was open for 4% of the time, Pallas kernels for 0%

commit v1 on v0

--- a/solution.py
+++ b/solution.py
@@ -60,7 +60,10 @@
             e_vir,
         )
         density = lax.dynamic_update_slice_in_dim(density, updated, offsets[step_index], 0)
-    return lax.all_to_all(density, "occ", split_axis=2, concat_axis=0, tiled=True)
+    return jnp.concatenate(
+        lax.all_to_all(jnp.stack(jnp.split(density, lax.axis_size("occ"), axis=2)), "occ", 0, 0),
+        axis=0,
+    )
 
 
 def solution(mesh):

time: 681 us -> 569 us (0.84)
  local copies, waits for them, and re-layouts: 120 us -> 36.5 us
  other arithmetic: 28.3 us -> 1.87 us
    unnamed x10 -> x16, local copies, waits for them, and re-layouts: 45.8 us -> 12.7 us
    all_to_all x1 -> x0, other arithmetic: 26.4 us -> none  [shards(): lax.all_to_all(density, 'occ', split_axis=2, concat_axis=0, tiled=True)]
    dynamic_update_slice x1 -> x0, local copies, waits for them, and re-layouts: 26.3 us -> none  [shards(): lax.dynamic_update_slice_in_dim(density, updated, offsets[step_index], 0)]
    all_to_all x2 -> x0, local copies, waits for them, and re-layouts: 25.6 us -> none  [shards(): lax.all_to_all(density, 'occ', split_axis=2, concat_axis=0, tiled=True)]
  transfers between devices with their start and end apart: 5 -> 5, of which waited for: 5 -> 5; matrix products, arithmetic and copies ran while one was open for 4% -> 5% of each run, Pallas kernels for 0% -> 0%
where the time goes in v1:
time: 569 us; the launch traced here: 568 us
  waiting for transfers between devices  362 us (64%)
  blocking collectives  98.3 us (17%)
  local copies, waits for them, and re-layouts  36.5 us (6%)
  matrix products  36.1 us (6%)
  between operations  26.4 us (5%)
  starting transfers between devices  6.32 us (1%)
    all_gather x3, waiting for transfers between devices, shards(): lax.all_gather(pair_slabs[step_index], 'vir', axis=0, tiled=True)  231 us
    all_to_all x1, blocking collectives, shards(): lax.all_to_all(jnp.stack(jnp.split(density, lax.axis_size('occ'), axis=2)...  98.3 us
    psum x1, waiting for transfers between devices, from_root(): return lax.psum(jnp.where(mine, shard, jnp.zeros_like(shard)), axis)  89 us
    all_to_all x1, waiting for transfers between devices, shards(): lax.all_to_all(factors, 'occ', split_axis=0, concat_axis=2, tiled=True)  41.5 us
    dot_general x3, matrix products, pair_terms(): jnp.einsum('iab,bp->iap', amplitude, column_piece, preferred_element_type...  36.1 us
    all_to_all x2, local copies, waits for them, and re-layouts, shards(): lax.all_to_all(factors, 'occ', split_axis=0, concat_axis=2, tiled=True)  15.9 us
    unnamed x16, local copies, waits for them, and re-layouts  12.7 us
  transfers between devices with their start and end apart: 5, of which 5 were waited for; matrix products, arithmetic and copies ran while one was open for 5% of the time, Pallas kernels for 0%

profile of v1, /device:TPU:1, one launch (start us, length us, event | category | flops | bytes accessed | tf_op | source)
XLA Modules:
  0.0 567.6 jit_solution(8713108653191267978)
XLA Ops:
  6.5 6.0 %all-to-all-start = ((bf16[256,32,256]{2,1,0:T(8,128)(2,1)}), bf16[256,32,256]{2,1,0:T(8,128)(2,1)}, u32[]{:S(2)}, u32[]{:S(2)}) async-start(bf16[256,32,256]{2,1,0:T(8,128)(2,1)} %param.5), calls=%async_computation | async-start | bytes 8388608 | tf_op jit(solution)/shard_map/all_to_all | solution.py:29
  20.7 41.5 %all-to-all-done = bf16[256,32,256]{2,1,0:T(8,128)(2,1)} async-done(((bf16[256,32,256]{2,1,0:T(8,128)(2,1)}), bf16[256,32,256]{2,1,0:T(8,128)(2,1)}, u32[]{:S(2)}, u32[]{:S(2)}) %all-to-all-start) | async-done | bytes 4194336 | tf_op jit(solution)/shard_map/all_to_all | solution.py:29
  62.2 8.5 %copy.8 = bf16[8,32,32,256]{3,0,2,1:T(8,128)(2,1)} copy(bf16[8,32,32,256]{3,2,1,0:T(8,128)(2,1)} %bitcast) | data formatting | bytes 8388608 | tf_op jit(solution)/shard_map/all_to_all | solution.py:29
  70.7 7.4 %all_to_all.19 = bf16[32,32,2048]{2,1,0:T(8,128)(2,1)} reshape(bf16[32,32,8,256]{3,2,1,0:T(8,128)(2,1)} %bitcast.88) | data formatting | bytes 8388608 | tf_op jit(solution)/shard_map/all_to_all | solution.py:29
  78.1 1.8 select_bitcast_fusion
  80.0 89.0 %all-reduce.3.cloned.1.call-done = (bf16[32,2048]{1,0:T(8,128)(2,1)}, bf16[32,2048]{1,0:T(8,128)(2,1)}, bf16[32,2048]{1,0:T(8,128)(2,1)}) async-done(((bf16[32,2048]{1,0:T(8,128)(2,1)}, bf16[32,2048]{1,0:T(8,128)(2,1)}, bf16[32,2048]{1,0:T(8,128)(2,1)}), (bf16[32,2048]{1,0:T(8,128)(2,1)}, bf16[32,2048]{1,0:T(8,128)(2,1)}, bf16[32,2048]{1,0:T(8,128)(2,1)})) %all-reduce.3.cloned.1.call-update) | async-done | bytes 393232 | tf_op jit(solution)/shard_map/psum | solution.py:12
  169.0 0.7 all-gather.6.cloned.1.call-update
  177.5 86.6 %all-gather.4.cloned.1.call-done = bf16[1024,2048]{1,0:T(8,128)(2,1)} async-done(((bf16[32,2048]{1,0:T(8,128)(2,1)}), bf16[1024,2048]{1,0:T(8,128)(2,1)}) %all-gather.4.cloned.1.call-update) | async-done | bytes 4194320 | tf_op jit(solution)/shard_map/all_gather | solution.py:59
  264.1 4.5 broadcast_in_dim.2
  268.6 11.3 %fusion.12 = f32[32,32,2048]{2,1,0:T(8,128)} fusion(f32[32,32,2048]{2,1,0:T(8,128)} %broadcast_in_dim.2, s32[]{:T(128)S(6)} %select_n.99, bf16[1024,2048]{1,0:T(8,128)(2,1)} %all-gather.4.cloned.1.call-done, bf16[32,32,2048]{2,1,0:T(8,128)(2,1)} %all_to_all.19, f32[]{:T(128)} %bitcast.6, f32[16]{0:T(128)S(1)} %get-tuple-element.13, ...), kind=kOutput, calls=%fused_computation.15 | convolution fusion | flops 4297588736 | bytes 14812736 | tf_op jit(solution)/shard_map/iab,bp->iap/dot_general | solution.py:23
  279.8 70.4 %all-gather.6.cloned.1.call-done = bf16[1024,2048]{1,0:T(8,128)(2,1)} async-done(((bf16[32,2048]{1,0:T(8,128)(2,1)}), bf16[1024,2048]{1,0:T(8,128)(2,1)}) %all-gather.6.cloned.1.call-update) | async-done | bytes 4194320 | tf_op jit(solution)/shard_map/all_gather | solution.py:59
  350.2 12.4 %add_dynamic-update-slice_fusion.1 = f32[32,32,2048]{2,1,0:T(8,128)} fusion(f32[32,32,2048]{2,1,0:T(8,128)} %fusion.12, s32[]{:T(128)S(6)} %select_n.109, bf16[1024,2048]{1,0:T(8,128)(2,1)} %all-gather.6.cloned.1.call-done, bf16[32,32,2048]{2,1,0:T(8,128)(2,1)} %all_to_all.19, f32[]{:T(128)} %bitcast.11, f32[16]{0:T(128)S(1)} %get-tuple-element.12, ...), kind=kOutput, calls=%fused_computation.14 | convolution fusion | flops 4298637312 | bytes 19007040 | tf_op jit(solution)/shard_map/iab,bp->iap/dot_general | solution.py:23
  362.6 73.5 %all-gather.8.cloned.1.call-done = bf16[1024,2048]{1,0:T(8,128)(2,1)} async-done(((bf16[32,2048]{1,0:T(8,128)(2,1)}), bf16[1024,2048]{1,0:T(8,128)(2,1)}) %all-gather.8.cloned.1.call-update) | async-done | bytes 4194320 | tf_op jit(solution)/shard_map/all_gather | solution.py:59
  436.1 12.5 %add_dynamic-update-slice_fusion = f32[32,32,2048]{2,1,0:T(8,128)} fusion(f32[32,32,2048]{2,1,0:T(8,128)} %add_dynamic-update-slice_fusion.1, s32[]{:T(128)S(6)} %select_n.118, bf16[1024,2048]{1,0:T(8,128)(2,1)} %all-gather.8.cloned.1.call-done, bf16[32,32,2048]{2,1,0:T(8,128)(2,1)} %all_to_all.19, f32[]{:T(128)} %bitcast.16, f32[16]{0:T(128)S(1)} %get-tuple-element.11, ...), kind=kOutput, calls=%fused_computation.13 | convolution fusion | flops 4298637312 | bytes 19007040 | tf_op jit(solution)/shard_map/iab,bp->iap/dot_general | solution.py:23
  448.6 1.3 fusion.53
  450.0 1.3 fusion.52
  451.3 1.3 fusion.51
  452.7 1.3 fusion.50
  454.0 1.3 fusion.49
  455.3 1.3 fusion.48
  456.7 1.3 fusion.47
  458.0 1.3 fusion.46
  459.3 98.3 %all_to_all.23 = f32[8,32,32,256]{3,2,1,0:T(8,128)S(1)} all-to-all(f32[8,32,32,256]{3,2,1,0:T(8,128)S(1)} %fusion.46), channel_id=1, replica_groups=mesh['occ'=8,'vir'=32] {'occ'}, dimensions={0} | all-to-all | bytes 16777216 | tf_op jit(solution)/shard_map/all_to_all | solution.py:64
  557.6 3.4 copy.23
  (21 shorter events, 2.9 us)
Async XLA Ops:
  6.5 6.0 %copy-start.1 = (s32[3]{0:T(128)S(1)}, s32[3]{0:T(128)}, u32[]{:S(2)}) copy-start(s32[3]{0:T(128)} %param.9) | copy-start | bytes 40
  6.5 55.7 %all-to-all-start = ((bf16[256,32,256]{2,1,0:T(8,128)(2,1)}), bf16[256,32,256]{2,1,0:T(8,128)(2,1)}, u32[]{:S(2)}, u32[]{:S(2)}) async-start(bf16[256,32,256]{2,1,0:T(8,128)(2,1)} %param.5), calls=%async_computation | async-start | bytes 8388608 | tf_op jit(solution)/shard_map/all_to_all | solution.py:29
  12.5 156.5 %all-reduce.3.cloned.1.call-start = ((), (), s32[]{:S(2)}) async-start(), calls=%async_computation.5 | async-start | bytes 786432 | tf_op jit(solution)/shard_map/psum | solution.py:12
  70.7 99.6 %copy-start.2 = (s32[3]{0:T(128)S(1)}, s32[3]{0:T(128)}, u32[]{:S(2)}) copy-start(s32[3]{0:T(128)} %param.8) | copy-start | bytes 40
  70.7 105.9 %copy-start.3 = (f32[1024]{0:T(1024)S(1)}, f32[1024]{0:T(1024)}, u32[]{:S(2)}) copy-start(f32[1024]{0:T(1024)} %param.7) | copy-start | bytes 12292
  70.7 106.0 %copy-start = (f32[256]{0:T(256)S(1)}, f32[256]{0:T(256)}, u32[]{:S(2)}) copy-start(f32[256]{0:T(256)} %param.6) | copy-start | bytes 3076
  79.9 184.2 %all-gather.4.cloned.1.call-start = ((), (), s32[]{:S(2)}) async-start(), calls=%async_computation.2 | async-start | bytes 4325376 | tf_op jit(solution)/shard_map/all_gather | solution.py:59
  169.0 181.2 %all-gather.6.cloned.1.call-start = ((), (), s32[]{:S(2)}) async-start(), calls=%async_computation.3 | async-start | bytes 4325376 | tf_op jit(solution)/shard_map/all_gather | solution.py:59
  169.7 266.4 %all-gather.8.cloned.1.call-start = ((), (), s32[]{:S(2)}) async-start(), calls=%async_computation.4 | async-start | bytes 4325376 | tf_op jit(solution)/shard_map/all_gather | solution.py:59
Sparse Core Ops, SparseCore 0:
  80.0 88.8 all-reduce.2
  171.8 92.3 all-gather.3
  266.9 83.2 all-gather.5
  352.8 83.2 all-gather.7
